TPU v7x, 256 devices: a whole 4x4x8 slice. The times are simulated.
256 devices in a mesh: dp: 64 (over x, z, core), rep: 4 (over y).
Axes of the slice: x: 4, y: 4, z: 8, core: 2. Of those that a mesh axis runs over, the one named last changes fastest.
Arguments:
- frames_in: bfloat16 [4, 57344, 1536], P('rep', 'dp')
- lengths: int32 [4, 64, 4], P('rep', 'dp'), may hold values from 1 to 893, as said below
- norm_gain: float32 [1536], replicated, may hold values from 0.5 to 1.5
- norm_bias: float32 [1536], replicated, may hold values from -2 to 2
- w_in: bfloat16 [1536, 3072], P(('dp', 'rep')), may hold values from -0.15625 to 0.15625
- kernel: float32 [31, 1536], replicated, may hold values from -1 to 1
- batch_gain: float32 [1536], replicated, may hold values from 0.5 to 1.5
- batch_bias: float32 [1536], replicated, may hold values from -3 to 3
- w_out: bfloat16 [1536, 1536], P(('dp', 'rep')), may hold values from -0.15625 to 0.15625
Outputs:
- frames_out: bfloat16 [4, 57344, 1536], P('rep', 'dp')
Inputs may be any that keep to these rules, and one draw needn't show every extreme that they name: `lengths`: for each rep index, the devices 2k and 2k + 1 of dp hold 1024 frames together, so each rep index holds 512 frames for each of its dp devices; a device holds at most 896 frames, and some device of every rep index holds exactly 896.
All inputs are finite; a program needn't handle non-finite values.
Results may differ from a plain program's by a relative error of at most 0.0038.
Values may be sent and summed in bfloat16 or wider, within the bound.
A program may use at most 128 MiB of HBM per device.

v0:
```python
import jax
import jax.numpy as jnp
from jax import lax
from jax.sharding import PartitionSpec as P

FR_DEV = 512
EPSILON = 1e-05


def layer_norm(frames, norm_gain, norm_bias):
    values = frames.astype(jnp.float32)
    average = jnp.mean(values, axis=-1, keepdims=True)
    centred = values - average
    spread = jnp.mean(centred * centred, axis=-1, keepdims=True)
    return centred * lax.rsqrt(spread + EPSILON) * norm_gain + norm_bias


def depthwise(gated, labels, kernel):
    half_kernel = kernel.shape[0] // 2
    length_rows = gated.shape[0]
    padded = jnp.pad(gated, ((half_kernel, half_kernel), (0, 0)))
    padded_labels = jnp.pad(labels, (half_kernel, half_kernel), constant_values=-1)
    summed = jnp.zeros(gated.shape, jnp.float32)
    for offset in range(kernel.shape[0]):
        shared = padded_labels[offset : offset + length_rows] == labels
        contribution = jnp.where(
            shared[:, None], padded[offset : offset + length_rows].astype(jnp.float32), 0.0
        )
        summed = summed + contribution * kernel[offset]
    return summed


def project_in(normed, weight_rows):
    return jnp.dot(normed, weight_rows, preferred_element_type=jnp.float32)


def project_out(active, weight_rows):
    return jnp.dot(active, weight_rows, preferred_element_type=jnp.float32)


def on_device(
    frames_in, lengths, norm_gain, norm_bias, w_in, kernel, batch_gain, batch_bias, w_out
):
    local_frames = frames_in[0]
    local_lengths = lengths[0, 0]
    capacity = local_frames.shape[0]
    features = local_frames.shape[1]
    total_count = lax.axis_size("dp") * lax.axis_size("rep") * FR_DEV
    grouped = (w_in, w_out)
    grouped = (
        lax.all_gather(w_in, ("dp", "rep"), axis=0, tiled=True),
        lax.all_gather(w_out, ("dp", "rep"), axis=0, tiled=True),
    )
    rows_here = jnp.arange(capacity, dtype=jnp.int32)
    local_load = jnp.sum(local_lengths)
    bounds = jnp.cumsum(local_lengths)
    labels = jnp.sum((rows_here[:, None] >= bounds[None, :]).astype(jnp.int32), axis=1)
    row_weight = (rows_here < local_load).astype(jnp.float32)[:, None]
    normed = layer_norm(local_frames, norm_gain, norm_bias).astype(jnp.bfloat16)
    projected = project_in(normed, grouped[0])
    gated = (projected[:, :features] * jax.nn.sigmoid(projected[:, features:])).astype(jnp.bfloat16)
    convolved = depthwise(gated, labels, kernel)
    average = lax.psum(jnp.sum(convolved * row_weight, axis=0), ("dp", "rep")) / total_count
    centred = convolved - average
    spread = lax.psum(jnp.sum(centred * centred * row_weight, axis=0), ("dp", "rep")) / total_count
    scaled = centred * lax.rsqrt(spread + EPSILON) * batch_gain + batch_bias
    active = jax.nn.silu(scaled).astype(jnp.bfloat16)
    branch = project_out(active, grouped[1])
    mixed = (local_frames.astype(jnp.float32) + branch).astype(jnp.bfloat16)
    result = jnp.where(rows_here[:, None] < local_load, mixed, jnp.zeros_like(mixed))
    return result[None]


def solution(mesh):
    placed = (
        P("rep", "dp", None),
        P("rep", "dp", None),
        P(),
        P(),
        P(("dp", "rep"), None),
        P(),
        P(),
        P(),
        P(("dp", "rep"), None),
    )
    return jax.shard_map(
        on_device, mesh=mesh, in_specs=placed, out_specs=P("rep", "dp", None), check_vma=False
    )
```

profile of v0, /device:TPU:1, one launch (start us, length us, event | category | flops | bytes accessed | tf_op | source)
XLA Modules:
  0.0 487.7 jit_solution(4124133330554323458)
XLA Ops:
  6.5 0.0 all-gather.7.cloned.1.call-start
  6.5 0.7 all-gather.7.cloned.1.call-update
  7.3 0.0 all-gather.5.cloned.1.call-start
  7.3 0.7 all-gather.5.cloned.1.call-update
  8.0 1.3 reduce_sum.54
  9.3 0.8 reduce-window.8
  10.1 0.6 iota_compare_fusion.1
  10.8 0.7 fusion.26
  11.4 0.1 convert_reduce_fusion.1
  11.5 1.5 slice_reduce_fusion.29
  13.0 1.8 slice_reduce_fusion.30
  14.9 0.1 slice_compare_fusion.26
  14.9 2.2 convert_reduce_fusion
  17.2 2.6 fusion.4
  19.8 0.1 slice_compare_fusion.29
  19.9 0.1 slice_compare_fusion.28
  20.0 0.1 slice_compare_fusion.27
  20.1 111.2 %all-gather.7.cloned.1.call-done = bf16[256,6,1536]{2,1,0:T(8,128)(2,1)} async-done(((bf16[1,6,1536]{2,1,0:T(8,128)(2,1)}), bf16[256,6,1536]{2,1,0:T(8,128)(2,1)}) %all-gather.7.cloned.1.call-update) | async-done | bytes 4718608 | tf_op jit(solution)/shard_map/all_gather | solution.py:52
  131.3 8.5 %reshape.87 = bf16[1536,1536]{1,0:T(8,128)(2,1)} reshape(bf16[256,6,1536]{2,1,0:T(8,128)(2,1)} %all-gather.7.cloned.1.call-done) | data formatting | bytes 9437184
  139.8 113.5 %all-gather.5.cloned.1.call-done = bf16[256,6,3072]{2,1,0:T(8,128)(2,1)} async-done(((bf16[1,6,3072]{2,1,0:T(8,128)(2,1)}), bf16[256,6,3072]{2,1,0:T(8,128)(2,1)}) %all-gather.5.cloned.1.call-update) | async-done | bytes 9437200 | tf_op jit(solution)/shard_map/all_gather | solution.py:51
  253.3 14.2 %reshape.85 = bf16[1536,3072]{1,0:T(8,128)(2,1)} reshape(bf16[256,6,3072]{2,1,0:T(8,128)(2,1)} %all-gather.5.cloned.1.call-done) | data formatting | bytes 18874368
  267.5 0.0 copy-done
  267.5 0.0 copy-done.2
  267.5 11.3 %fusion.16 = f32[896,3072]{1,0:T(8,128)S(1)} fusion(bf16[1536,3072]{1,0:T(8,128)(2,1)} %reshape.85, bf16[1,896,1536]{2,1,0:T(8,128)(2,1)S(1)} %copy-done, f32[1536]{0:T(1024)S(1)} %copy-done.2, f32[1536]{0:T(1024)S(1)} %copy-done.3, f32[896]{0:T(1024)S(1)} %add_rsqrt_fusion.1, f32[896]{0:T(1024)S(1)} %broadcast_multiply_fusion.1), kind=kOutput, calls=%fused_computation.23 | convolution fusion | flops 8463974400 | bytes 23219200 | tf_op jit(solution)/shard_map/dot_general | solution.py:34
  278.8 1.5 fusion.13
  280.4 0.0 copy-start.4
  280.4 0.0 copy-start.5
  280.4 38.3 %multiply_reduce_fusion.1 = (f32[1536]{0:T(1024)S(1)}, f32[896,1536]{1,0:T(8,128)}) fusion(f32[896]{0:T(1024)S(1)} %fusion.26, f32[1536]{0:T(1024)S(1)} %get-tuple-element.34, pred[896]{0:T(1024)(128)(4,1)S(1)} %get-tuple-element.67, f32[1536]{0:T(1024)S(1)} %get-tuple-element.35, pred[896]{0:T(1024)(128)(4,1)S(1)} %get-tuple-element.39, ...), kind=kLoop, calls=%fused_computation.18 | loop fusion | flops 170654208 | bytes 8484608 | tf_op jit(solution)/shard_map/reduce_sum | solution.py:63
  318.7 74.8 %psum.14 = f32[1536]{0:T(1024)S(1)} all-reduce(f32[1536]{0:T(1024)S(1)} %get-tuple-element.36), channel_id=1, replica_groups=mesh['dp'=64,'rep'=4] {'dp','rep'}, use_global_device_ids=true, to_apply=%region_6.7 | all-reduce | flops 1536 | bytes 12288 | tf_op jit(solution)/shard_map/psum | solution.py:63
  393.5 3.3 multiply_reduce_fusion
  396.8 73.6 %psum.15 = f32[1536]{0:T(1024)S(1)} all-reduce(f32[1536]{0:T(1024)S(1)} %multiply_reduce_fusion), channel_id=1, replica_groups=mesh['dp'=64,'rep'=4] {'dp','rep'}, use_global_device_ids=true, to_apply=%region_8.9 | all-reduce | flops 1536 | bytes 12288 | tf_op jit(solution)/shard_map/psum | solution.py:65
  470.4 10.4 %fusion.15 = bf16[1,896,1536]{2,1,0:T(8,128)(2,1)} fusion(bf16[1536,1536]{1,0:T(8,128)(2,1)} %reshape.87, bf16[1,896,1536]{2,1,0:T(8,128)(2,1)S(1)} %copy-done.1, f32[896,1536]{1,0:T(8,128)} %get-tuple-element.37, f32[1536]{0:T(1024)S(1)} %copy-done.4, f32[1536]{0:T(1024)S(1)} %copy-done.5, f32[1536]{0:T(1024)S(1)} %add_rsqrt_fusion, ...), kind=kOutput, calls=%fused_computation.22 | convolution fusion | flops 4245749760 | bytes 15754112 | tf_op jit(solution)/shard_map/dot_general | solution.py:38
  (12 shorter events, 0.0 us)
Async XLA Ops:
  6.5 124.8 %all-gather.7.cloned.1.call-start = ((), (), s32[]{:S(2)}) async-start(), calls=%async_computation.1 | async-start | bytes 6316032 | tf_op jit(solution)/shard_map/all_gather | solution.py:52
  7.3 246.1 %all-gather.5.cloned.1.call-start = ((), (), s32[]{:S(2)}) async-start(), calls=%async_computation | async-start | bytes 12632064 | tf_op jit(solution)/shard_map/all_gather | solution.py:51
  139.8 127.7 %copy-start = (bf16[1,896,1536]{2,1,0:T(8,128)(2,1)S(1)}, bf16[1,896,1536]{2,1,0:T(8,128)(2,1)}, u32[]{:S(2)}) copy-start(bf16[1,896,1536]{2,1,0:T(8,128)(2,1)} %param.9) | copy-start | bytes 8257540
  139.8 127.7 %copy-start.2 = (f32[1536]{0:T(1024)S(1)}, f32[1536]{0:T(1024)}, u32[]{:S(2)}) copy-start(f32[1536]{0:T(1024)} %param.12) | copy-start | bytes 18436
  139.8 127.7 %copy-start.3 = (f32[1536]{0:T(1024)S(1)}, f32[1536]{0:T(1024)}, u32[]{:S(2)}) copy-start(f32[1536]{0:T(1024)} %param.11) | copy-start | bytes 18436
  280.4 190.1 %copy-start.4 = (f32[1536]{0:T(1024)S(1)}, f32[1536]{0:T(1024)}, u32[]{:S(2)}) copy-start(f32[1536]{0:T(1024)} %param.16) | copy-start | bytes 18436
  280.4 190.1 %copy-start.5 = (f32[1536]{0:T(1024)S(1)}, f32[1536]{0:T(1024)}, u32[]{:S(2)}) copy-start(f32[1536]{0:T(1024)} %param.15) | copy-start | bytes 18436
  318.7 151.7 %copy-start.1 = (bf16[1,896,1536]{2,1,0:T(8,128)(2,1)S(1)}, bf16[1,896,1536]{2,1,0:T(8,128)(2,1)}, u32[]{:S(2)}) copy-start(bf16[1,896,1536]{2,1,0:T(8,128)(2,1)} %param.9) | copy-start | bytes 8257540
Sparse Core Ops, SparseCore 0:
  11.2 120.0 all-gather.6
  135.1 118.1 all-gather.4
where the time goes:
time: 489 us; the launch traced here: 488 us
  waiting for transfers between devices  226 us (46%)
  blocking collectives  148 us (30%)
  other arithmetic  51.8 us (11%)
  local copies, waits for them, and re-layouts  26 us (5%)
  matrix products  21.8 us (4%)
  between operations  13.5 us (3%)
    all_gather x1, waiting for transfers between devices, on_device(): lax.all_gather(w_in, ('dp', 'rep'), axis=0, tiled=True)  114 us
    all_gather x1, waiting for transfers between devices, on_device(): lax.all_gather(w_out, ('dp', 'rep'), axis=0, tiled=True)  111 us
    psum x1, blocking collectives, on_device(): lax.psum(jnp.sum(convolved * row_weight, axis=0), ('dp', 'rep'))  74.8 us
    psum x1, blocking collectives, on_device(): lax.psum(jnp.sum(centred * centred * row_weight, axis=0), ('dp', 'rep'))  73.6 us
    reduce_sum x1, other arithmetic, on_device(): jnp.sum(convolved * row_weight, axis=0)  38.3 us
    unnamed x14, local copies, waits for them, and re-layouts  22.6 us
    dot_general x1, matrix products, project_in(): return jnp.dot(normed, weight_rows, preferred_element_type=jnp.float32)  11.3 us
    dot_general x1, matrix products, project_out(): return jnp.dot(active, weight_rows, preferred_element_type=jnp.float32)  10.4 us
  transfers between devices with their start and end apart: 2, of which 2 were waited for; matrix products, arithmetic and copies ran while one was open for 4% of the time, Pallas kernels for 0%

commit v1 on v0

--- a/solution.py
+++ b/solution.py
@@ -2,6 +2,7 @@
 import jax.numpy as jnp
 from jax import lax
 from jax.sharding import PartitionSpec as P
+from jax.lax import all_gather
 
 FR_DEV = 512
 EPSILON = 1e-05
@@ -60,7 +61,9 @@
     projected = project_in(normed, grouped[0])
     gated = (projected[:, :features] * jax.nn.sigmoid(projected[:, features:])).astype(jnp.bfloat16)
     convolved = depthwise(gated, labels, kernel)
-    average = lax.psum(jnp.sum(convolved * row_weight, axis=0), ("dp", "rep")) / total_count
+    average = (
+        jnp.sum(all_gather(jnp.sum(convolved * row_weight, axis=0), ("dp", "rep")), 0) / total_count
+    )
     centred = convolved - average
     spread = lax.psum(jnp.sum(centred * centred * row_weight, axis=0), ("dp", "rep")) / total_count
     scaled = centred * lax.rsqrt(spread + EPSILON) * batch_gain + batch_bias

time: 489 us -> 458 us (0.937)
  blocking collectives: 148 us -> 77.1 us
  waiting for transfers between devices: 226 us -> 264 us
    all_gather x0 -> x1, waiting for transfers between devices: none -> 95.6 us  [on_device(): all_gather(jnp.sum(convolved * row_weight, axis=0), ('dp', 'rep'))]
    psum x1 -> x0, blocking collectives: 74.8 us -> none  [on_device(): lax.psum(jnp.sum(convolved * row_weight, axis=0), ('dp', 'rep'))]
    all_gather x1, waiting for transfers between devices: 111 us -> 50.2 us  [on_device(): lax.all_gather(w_out, ('dp', 'rep'), axis=0, tiled=True)]
    unnamed x14 -> x17, local copies, waits for them, and re-layouts: 22.6 us -> 23.2 us
  transfers between devices with their start and end apart: 2 -> 3, of which waited for: 2 -> 3; matrix products, arithmetic and copies ran while one was open for 4% -> 19% of each run, Pallas kernels for 0% -> 0%
where the time goes in v1:
time: 458 us; the launch traced here: 457 us
  waiting for transfers between devices  264 us (58%)
  blocking collectives  77.1 us (17%)
  other arithmetic  53.6 us (12%)
  local copies, waits for them, and re-layouts  26.6 us (6%)
  matrix products  21.8 us (5%)
  between operations  13.2 us (3%)
    all_gather x1, waiting for transfers between devices, on_device(): lax.all_gather(w_in, ('dp', 'rep'), axis=0, tiled=True)  117 us
    all_gather x1, waiting for transfers between devices, on_device(): all_gather(jnp.sum(convolved * row_weight, axis=0), ('dp', 'rep'))  95.6 us
    psum x1, blocking collectives, on_device(): lax.psum(jnp.sum(centred * centred * row_weight, axis=0), ('dp', 'rep'))  77.1 us
    all_gather x1, waiting for transfers between devices, on_device(): lax.all_gather(w_out, ('dp', 'rep'), axis=0, tiled=True)  50.2 us
    reduce_sum x1, other arithmetic, on_device(): jnp.sum(convolved * row_weight, axis=0)  38.3 us
    unnamed x17, local copies, waits for them, and re-layouts  23.2 us
    dot_general x1, matrix products, project_in(): return jnp.dot(normed, weight_rows, preferred_element_type=jnp.float32)  11.3 us
    dot_general x1, matrix products, project_out(): return jnp.dot(active, weight_rows, preferred_element_type=jnp.float32)  10.5 us
  transfers between devices with their start and end apart: 3, of which 3 were waited for; matrix products, arithmetic and copies ran while one was open for 19% of the time, Pallas kernels for 0%

profile of v1, /device:TPU:1, one launch (start us, length us, event | category | flops | bytes accessed | tf_op | source)
XLA Modules:
  0.0 456.7 jit_solution(2228662240689349698)
XLA Ops:
  6.5 0.7 all-gather.8.cloned.1.call-update
  7.3 0.0 all-gather.12.cloned.1.call-start
  7.3 0.7 all-gather.12.cloned.1.call-update
  8.0 0.0 all-gather.10.cloned.1.call-start
  8.1 1.9 slice_reduce_fusion.30
  9.9 0.8 reduce-window.8
  10.7 0.1 convert_reduce_fusion.1
  10.8 0.1 slice_compare_fusion.26
  10.9 2.2 convert_reduce_fusion
  13.1 2.6 fusion.4
  15.8 1.6 slice_reduce_fusion.29
  17.3 0.7 reduce_sum.63
  18.0 0.7 fusion.26
  18.7 0.1 slice_compare_fusion.29
  18.8 0.1 slice_compare_fusion.28
  18.9 0.1 slice_compare_fusion.27
  19.0 0.0 copy-start.3
  19.0 117.1 %all-gather.8.cloned.1.call-done = bf16[256,6,3072]{2,1,0:T(8,128)(2,1)} async-done(((bf16[1,6,3072]{2,1,0:T(8,128)(2,1)}), bf16[256,6,3072]{2,1,0:T(8,128)(2,1)}) %all-gather.8.cloned.1.call-update) | async-done | bytes 9437200 | tf_op jit(solution)/shard_map/all_gather | solution.py:52
  136.1 14.2 %reshape.88 = bf16[1536,3072]{1,0:T(8,128)(2,1)} reshape(bf16[256,6,3072]{2,1,0:T(8,128)(2,1)} %all-gather.8.cloned.1.call-done) | data formatting | bytes 18874368
  150.3 11.3 %fusion.16 = f32[896,3072]{1,0:T(8,128)S(1)} fusion(bf16[1536,3072]{1,0:T(8,128)(2,1)} %reshape.88, bf16[1,896,1536]{2,1,0:T(8,128)(2,1)S(1)} %copy-done, f32[1536]{0:T(1024)S(1)} %copy-done.2, f32[1536]{0:T(1024)S(1)} %copy-done.3, f32[896]{0:T(1024)S(1)} %add_rsqrt_fusion.1, f32[896]{0:T(1024)S(1)} %broadcast_multiply_fusion.1), kind=kOutput, calls=%fused_computation.23 | convolution fusion | flops 8463974400 | bytes 23219200 | tf_op jit(solution)/shard_map/dot_general | solution.py:35
  161.6 1.5 fusion.13
  163.1 38.3 %multiply_reduce_fusion.1 = (f32[1536]{0:T(1024)S(1)}, f32[896,1536]{1,0:T(8,128)}) fusion(f32[896]{0:T(1024)S(1)} %fusion.26, f32[1536]{0:T(1024)S(1)} %get-tuple-element.34, pred[896]{0:T(1024)(128)(4,1)S(1)} %get-tuple-element.67, f32[1536]{0:T(1024)S(1)} %get-tuple-element.35, pred[896]{0:T(1024)(128)(4,1)S(1)} %get-tuple-element.39, ...), kind=kLoop, calls=%fused_computation.18 | loop fusion | flops 170654208 | bytes 8484608 | tf_op jit(solution)/shard_map/reduce_sum | solution.py:65
  201.5 0.6 reshape.89
  202.1 0.0 all-gather.10.cloned.1.call-update
  202.1 0.7 iota_compare_fusion.1
  202.8 50.2 %all-gather.12.cloned.1.call-done = bf16[256,6,1536]{2,1,0:T(8,128)(2,1)} async-done(((bf16[1,6,1536]{2,1,0:T(8,128)(2,1)}), bf16[256,6,1536]{2,1,0:T(8,128)(2,1)}) %all-gather.12.cloned.1.call-update) | async-done | bytes 4718608 | tf_op jit(solution)/shard_map/all_gather | solution.py:53
  253.0 8.4 %reshape.92 = bf16[1536,1536]{1,0:T(8,128)(2,1)} reshape(bf16[256,6,1536]{2,1,0:T(8,128)(2,1)} %all-gather.12.cloned.1.call-done) | data formatting | bytes 9437184
  261.4 95.6 %all-gather.10.cloned.1.call-done = f32[256,1,1536]{2,1,0:T(1,128)} async-done(((f32[1,1,1536]{2,1,0:T(1,128)}), f32[256,1,1536]{2,1,0:T(1,128)}) %all-gather.10.cloned.1.call-update) | async-done | bytes 1572880 | tf_op jit(solution)/shard_map/all_gather | solution.py:65
  357.0 2.3 reduce_sum.68
  359.3 3.3 multiply_reduce_fusion
  362.6 77.1 %psum.7 = f32[1536]{0:T(1024)S(1)} all-reduce(f32[1536]{0:T(1024)S(1)} %multiply_reduce_fusion), channel_id=1, replica_groups=mesh['dp'=64,'rep'=4] {'dp','rep'}, use_global_device_ids=true, to_apply=%region_8.9 | all-reduce | flops 1536 | bytes 12288 | tf_op jit(solution)/shard_map/psum | solution.py:68
  439.7 10.5 %fusion.15 = bf16[1,896,1536]{2,1,0:T(8,128)(2,1)} fusion(bf16[1536,1536]{1,0:T(8,128)(2,1)} %reshape.92, bf16[1,896,1536]{2,1,0:T(8,128)(2,1)S(1)} %copy-done.1, f32[896,1536]{1,0:T(8,128)} %get-tuple-element.37, f32[1536]{0:T(1024)S(1)} %copy-done.4, f32[1536]{0:T(1024)S(1)} %copy-done.5, f32[1536]{0:T(1024)S(1)} %add_rsqrt_fusion, ...), kind=kOutput, calls=%fused_computation.22 | convolution fusion | flops 4245749760 | bytes 15754112 | tf_op jit(solution)/shard_map/dot_general | solution.py:39
  (18 shorter events, 0.1 us)
Async XLA Ops:
  6.5 10.8 %copy-start.6 = (s32[1,1,4]{2,1,0:T(1,128)S(1)}, s32[1,1,4]{2,1,0:T(1,128)}, u32[]{:S(2)}) copy-start(s32[1,1,4]{2,1,0:T(1,128)} %param.10) | copy-start | bytes 52
  6.5 129.5 %all-gather.8.cloned.1.call-start = ((), (), s32[]{:S(2)}) async-start(), calls=%async_computation | async-start | bytes 12632064 | tf_op jit(solution)/shard_map/all_gather | solution.py:52
  7.3 245.7 %all-gather.12.cloned.1.call-start = ((), (), s32[]{:S(2)}) async-start(), calls=%async_computation.2 | async-start | bytes 6316032 | tf_op jit(solution)/shard_map/all_gather | solution.py:53
  8.0 349.0 %all-gather.10.cloned.1.call-start = ((), (), s32[]{:S(2)}) async-start(), calls=%async_computation.1 | async-start | bytes 1579008 | tf_op jit(solution)/shard_map/all_gather | solution.py:65
  19.0 131.3 %copy-start = (bf16[1,896,1536]{2,1,0:T(8,128)(2,1)S(1)}, bf16[1,896,1536]{2,1,0:T(8,128)(2,1)}, u32[]{:S(2)}) copy-start(bf16[1,896,1536]{2,1,0:T(8,128)(2,1)} %param.9) | copy-start | bytes 8257540
  19.0 131.3 %copy-start.2 = (f32[1536]{0:T(1024)S(1)}, f32[1536]{0:T(1024)}, u32[]{:S(2)}) copy-start(f32[1536]{0:T(1024)} %param.12) | copy-start | bytes 18436
  19.0 131.2 %copy-start.3 = (f32[1536]{0:T(1024)S(1)}, f32[1536]{0:T(1024)}, u32[]{:S(2)}) copy-start(f32[1536]{0:T(1024)} %param.11) | copy-start | bytes 18436
  261.4 178.3 %copy-start.1 = (bf16[1,896,1536]{2,1,0:T(8,128)(2,1)S(1)}, bf16[1,896,1536]{2,1,0:T(8,128)(2,1)}, u32[]{:S(2)}) copy-start(bf16[1,896,1536]{2,1,0:T(8,128)(2,1)} %param.9) | copy-start | bytes 8257540
  261.4 178.3 %copy-start.4 = (f32[1536]{0:T(1024)S(1)}, f32[1536]{0:T(1024)}, u32[]{:S(2)}) copy-start(f32[1536]{0:T(1024)} %param.16) | copy-start | bytes 18436
  261.4 178.3 %copy-start.5 = (f32[1536]{0:T(1024)S(1)}, f32[1536]{0:T(1024)}, u32[]{:S(2)}) copy-start(f32[1536]{0:T(1024)} %param.15) | copy-start | bytes 18436
Sparse Core Ops, SparseCore 0:
  11.2 124.8 all-gather.7
  139.9 113.0 all-gather.11
  256.7 100.2 all-gather.9
